TPU v7x, 32 devices: a whole 2x2x4 slice. The times are simulated.
32 devices in a mesh: cuts: 1, mode: 32 (over z, y, x, core).
Axes of the slice: x: 2, y: 2, z: 4, core: 2. Of those that a mesh axis runs over, the one named last changes fastest.
Arguments:
- branch_in: bfloat16 [4, 2, 2048, 1024], P(None, None, ('cuts', 'mode')), may hold values from -6 to 6
- column_order: int32 [4, 1024], replicated, may hold values from 0 to 1023, each once within a row
- gate_a: bfloat16 [2, 1024, 1024], P(None, 'mode'), may hold values from -0.125 to 0.125
- gate_b: bfloat16 [2, 1024, 1024], P(None, 'mode'), may hold values from -0.125 to 0.125
Outputs:
- joined: bfloat16 [2, 512, 2, 128], P(None, ('cuts', 'mode'))
Inputs may be any that keep to these rules, and one draw needn't show every extreme that they name: Each row of column_order names every column state once.
All inputs are finite; a program needn't handle non-finite values.
Results may differ from a plain program's by a relative error of at most 0.014.
Values may be sent and summed in bfloat16 or wider, within the bound.
A program may use at most 128 MiB of HBM per device.

v0:
```python
import jax
import jax.numpy as jnp
from jax import lax
from jax.experimental import pallas as pl
from jax.experimental.pallas import tpu as pltpu
from jax.sharding import PartitionSpec as P

SHARED = 4096
KEPT = 4
CYCLES = 2
F32 = jnp.float32
BF16 = jnp.bfloat16


def complex_dot(left_real, left_imag, right_real, right_imag):
    real_part = jnp.dot(left_real, right_real, preferred_element_type=F32) - jnp.dot(
        left_imag, right_imag, preferred_element_type=F32
    )
    imag_part = jnp.dot(left_real, right_imag, preferred_element_type=F32) + jnp.dot(
        left_imag, right_real, preferred_element_type=F32
    )
    return real_part, imag_part


def layers_plain(state, orders, whole_a, whole_b):
    parts, devices, sides, share, width = state.shape
    group = width // devices
    iota = lax.broadcasted_iota(jnp.int32, (width, width), 0)
    halves = []
    for side in range(sides):
        one_hot = (iota == orders[side][None, :]).astype(BF16)
        piece = state[:, :, side].reshape(parts * devices * share, width)
        halves.append(
            jnp.dot(piece, one_hot, preferred_element_type=F32)
            .astype(BF16)
            .reshape(parts, devices, share, width)
        )
    state = jnp.stack(halves, axis=2)
    for layer in range(2 * CYCLES):
        if layer > 0:
            pieces = state.reshape(parts, devices, sides, share, devices, group)
            state = pieces.transpose(0, 4, 2, 3, 1, 5)
        flat = state.reshape(parts, devices * sides * share, width)
        gate = whole_a if layer % 2 == 0 else whole_b
        state = jnp.stack(complex_dot(flat[0], flat[1], gate[0], gate[1])).astype(BF16)
    return state.reshape(parts, devices, sides, share, width)


LANES = 128
HIGH = 8


def swap_lane_blocks(blocks, group):
    count = len(blocks)
    lane = lax.broadcasted_iota(jnp.int32, (HIGH, LANES), 1) // group
    bit = count // 2
    while bit:
        low = (lane // bit) % 2 == 0
        new = list(blocks)
        for i in range(count):
            if i & bit == 0:
                first, second = blocks[i], blocks[i | bit]
                new[i] = jnp.where(low, first, pltpu.roll(second, bit * group, 1))
                new[i | bit] = jnp.where(low, pltpu.roll(first, LANES - bit * group, 1), second)
        blocks = new
        bit //= 2
    return blocks


def whole_kernel(
    devices,
    dealt,
    orders,
    gate_a,
    gate_b,
    out,
    gates,
    landed,
    state,
    product,
    hot,
    mixer,
    left_out,
    right_out,
    left_in,
    right_in,
    part_out,
    part_in,
    own_sem,
    deal_send,
    deal_recv,
    gate_send,
    gate_recv,
    left_send,
    left_recv,
    right_send,
    right_recv,
    part_send,
    part_recv,
):
    me = lax.axis_index("mode")
    width = dealt.shape[2]
    rows = state.shape[1]
    groups = width // devices
    packed = LANES // groups
    holders = KEPT
    quarter = SHARED // width
    share = HIGH // 2
    barrier = pltpu.get_barrier_semaphore()

    def greet(o, carry):
        pl.semaphore_signal(barrier, inc=1, device_id={"mode": me ^ o})
        return carry

    lax.fori_loop(1, devices, greet, 0)

    def remote(src, dst, ssem, rsem, target):
        return pltpu.make_async_remote_copy(
            src_ref=src,
            dst_ref=dst,
            send_sem=ssem,
            recv_sem=rsem,
            device_id={"mode": target},
            device_id_type=pl.DeviceIdType.MESH,
        )

    z1, z0, y, x, c = (me // 16, me // 8 % 2, me // 4 % 2, me // 2 % 2, me % 2)
    every = slice(None)
    shards = (gate_a, gate_b)
    own = [
        pltpu.make_async_copy(shards[g], gates.at[g, :, z1, z0, y, x, c], own_sem.at[g])
        for g in range(2)
    ]
    own_x = pltpu.make_async_copy(dealt.at[me], landed.at[me], own_sem.at[2])
    for copy in own + [own_x]:
        copy.start()

    def region(g, part, index):
        return gates.at[(g, part) + index]

    steps = {
        "z0": (every, (z1, z0, y, x, c), 8),
        "z1": (every, (z1, every, y, x, c), 16),
        "p0": (0, (every, every, y, x, c), 4),
        "p1": (1, (every, every, y, x, c), 2),
        "q0": (0, (every, every, every, x, c), 2),
        "q1": (1, (every, every, y, every, c), 4),
        "c0": (every, (every, every, y, x, c), 1),
        "d0": (0, (every, every, 1 - y, x, c), 1),
        "d1": (1, (every, every, y, 1 - x, c), 1),
        "e0": (0, (every, every, every, 1 - x, c), 1),
        "e1": (1, (every, every, 1 - y, every, c), 1),
    }
    names = list(steps)

    def gate_copy(g, name):
        part, index, bit = steps[name]
        k = names.index(name)
        here = region(g, part, index)
        src = shards[g] if name == "z0" else here
        return remote(src, here, gate_send.at[g, k], gate_recv.at[g, k], me ^ bit)

    def send(g, *which):
        for name in which:
            gate_copy(g, name).start()

    def arrive(g, *which):
        for name in which:
            gate_copy(g, name).wait_recv()

    def deal_copy(o):
        return remote(dealt.at[me ^ o], landed.at[me], deal_send.at[o], deal_recv.at[o], me ^ o)

    def start_deal(o, carry):
        deal_copy(o).start()
        return carry

    pl.semaphore_wait(barrier, devices - 1)
    send(0, "z0")
    send(1, "z0")
    lax.fori_loop(1, 8, start_deal, 0)
    k = lax.broadcasted_iota(jnp.int32, (width, width), 1)
    natural = (
        (k % 32 // share) * 128 + (k // 64 % 4) * 32 + (k % share) * 8 + (k // 256) * 2 + k // 32 % 2
    )
    for copy in own:
        copy.wait()
    arrive(0, "z0")
    send(0, "z1")
    arrive(1, "z0")
    send(1, "z1")
    lax.fori_loop(8, devices, start_deal, 0)
    mixer[...] = jnp.where(
        lax.broadcasted_iota(jnp.int32, (width, width), 0) == natural, 1.0, 0.0
    ).astype(BF16)
    arrive(0, "z1")
    send(0, "p0", "p1", "c0")
    arrive(1, "z1")
    send(1, "p0", "p1", "c0")
    arrive(0, "p0", "p1")
    send(0, "q0", "q1", "d0", "d1")
    arrive(1, "p0", "p1")
    send(1, "q0", "q1", "d0", "d1")

    own_x.wait()

    def wait_deal(o, carry):
        remote(dealt.at[me], landed.at[me ^ o], deal_send.at[o], deal_recv.at[o], me ^ o).wait_recv()
        return carry

    lax.fori_loop(1, devices, wait_deal, 0)
    wide = landed[...].astype(F32)
    for part in range(2):
        state[part] = wide[:, part * HIGH : (part + 1) * HIGH].reshape(rows, width).astype(BF16)
    first_side = lax.broadcasted_iota(jnp.int32, (rows, width // 4), 0) % HIGH < share
    for side in range(2):
        source = lax.broadcasted_iota(jnp.int32, (width, width), 0)
        hot[side] = jnp.where(source == orders[side : side + 1, :], 1.0, 0.0).astype(BF16)

    def tile_of(n):
        return pl.ds(pl.multiple_of(n * (width // 4), width // 4), width // 4)

    @pl.loop(0, 4)
    def _(n):
        cols = tile_of(n)
        for part in range(2):
            one = jnp.dot(state[part], hot[0, :, cols], preferred_element_type=F32)
            two = jnp.dot(state[part], hot[1, :, cols], preferred_element_type=F32)
            product[part, :, cols] = jnp.where(first_side, one, two)

    for part in range(2):
        state[part] = product[part].astype(BF16)

    def layer(g):
        @pl.loop(0, 4)
        def _(n):
            cols = tile_of(n)
            real = gates[g, 0, :, :, :, :, :, :, cols].reshape(width, width // 4)
            imag = gates[g, 1, :, :, :, :, :, :, cols].reshape(width, width // 4)
            real_part, imag_part = complex_dot(state[0], state[1], real, imag)
            product[0, :, cols] = real_part
            product[1, :, cols] = imag_part

    def regroup():
        span = packed * HIGH

        @pl.loop(0, devices // packed)
        def _(a):
            base = pl.multiple_of(a * span, span)
            cols = pl.ds(pl.multiple_of(a * LANES, LANES), LANES)
            for part in range(2):
                for s in range(width // LANES):
                    block = product[part, pl.ds(base, span), s * LANES : (s + 1) * LANES]
                    blocks = [block[i * HIGH : (i + 1) * HIGH] for i in range(packed)]
                    blocks = swap_lane_blocks(blocks, groups)
                    state[part, s * span : (s + 1) * span, cols] = jnp.concatenate(
                        blocks, axis=0
                    ).astype(BF16)

    arrive(0, "q0", "q1")
    send(0, "e0", "e1")
    arrive(0, "c0", "d0", "d1", "e0", "e1")
    layer(0)
    regroup()
    arrive(1, "q0", "q1")
    send(1, "e0", "e1")
    arrive(1, "c0", "d0", "d1", "e0", "e1")
    layer(1)
    for number in range(2, 2 * CYCLES):
        regroup()
        layer(number % 2)

    upper = lax.broadcasted_iota(jnp.int32, (HIGH, width), 0) < share

    @pl.loop(0, devices // 4)
    def _(r):
        base = pl.multiple_of(r * 4 * HIGH, 4 * HIGH)
        to = pl.ds(pl.multiple_of(r * 4 * share, 4 * share), 4 * share)
        for part in range(2):
            slab = product[part, pl.ds(base, 4 * HIGH)]
            lines = [slab[i * HIGH : (i + 1) * HIGH] for i in range(4)]
            lefts, rights = [], []
            for i in range(0, 4, 2):
                lefts.append(jnp.where(upper, lines[i], pltpu.roll(lines[i + 1], share, 0)))
                rights.append(jnp.where(upper, pltpu.roll(lines[i], share, 0), lines[i + 1]))
            left_out[part, to] = jnp.concatenate(lefts, axis=0).astype(BF16)
            right = jnp.concatenate(rights, axis=0).astype(BF16)
            for block in range(width // LANES):
                right_out[part, block // KEPT, block % KEPT, to] = right[
                    :, block * LANES : (block + 1) * LANES
                ]

    lot = left_out.shape[1] // KEPT
    in_pair = quarter * holders
    slot = me % in_pair
    hold = me % holders

    def lot_of(i):
        return pl.ds(pl.multiple_of(i * lot, lot), lot)

    def right_copy(o):
        target = slot ^ o
        return remote(
            right_out.at[:, :, target % holders, lot_of(target // holders)],
            right_in.at[slot],
            right_send.at[o],
            right_recv.at[o],
            me ^ o,
        )

    def right_wait(o):
        return remote(
            right_out.at[:, :, 0, lot_of(0)],
            right_in.at[slot ^ o],
            right_send.at[o],
            right_recv.at[o],
            me ^ o,
        )

    def left_copy(o):
        return remote(
            left_out.at[:, lot_of(hold ^ o)],
            left_in.at[:, hold],
            left_send.at[o],
            left_recv.at[o],
            me ^ o,
        )

    def left_wait(o):
        return remote(
            left_out.at[:, lot_of(0)],
            left_in.at[:, hold ^ o],
            left_send.at[o],
            left_recv.at[o],
            me ^ o,
        )

    def start_right(o, carry):
        right_copy(o).start()
        return carry

    lax.fori_loop(4, in_pair, start_right, 0)
    for o in range(1, holders):
        left_copy(o).start()
    lax.fori_loop(1, 4, start_right, 0)
    own_left = pltpu.make_async_copy(
        left_out.at[:, lot_of(hold)], left_in.at[:, hold], own_sem.at[3]
    )
    own_right = pltpu.make_async_copy(
        right_out.at[:, :, slot % holders, lot_of(slot // holders)], right_in.at[slot], own_sem.at[4]
    )
    own_left.start()
    own_right.start()
    own_left.wait()
    own_right.wait()
    for o in range(1, holders):
        left_wait(o).wait_recv()

    def end_right(o, carry):
        right_wait(o).wait_recv()
        return carry

    lax.fori_loop(1, in_pair, end_right, 0)
    arrived = right_in[...]
    both = jnp.concatenate(
        [arrived[:, part].reshape(width, LANES) for part in range(2)], axis=1
    )
    both = jnp.dot(mixer[...], both, preferred_element_type=F32).astype(BF16)
    by_real = jnp.dot(
        left_in[0].reshape(KEPT * lot, width), both, preferred_element_type=F32
    )
    by_imag = jnp.dot(
        left_in[1].reshape(KEPT * lot, width), both, preferred_element_type=F32
    )
    partial = jnp.concatenate(
        [
            by_real[:, :LANES] - by_imag[:, LANES:],
            by_real[:, LANES:] + by_imag[:, :LANES],
        ],
        axis=1,
    )
    top = lax.broadcasted_iota(jnp.int32, (HIGH, 2 * LANES), 0) < share
    for m in range(0, lot // share, 2):
        lines = [partial[h * lot + m * share : h * lot + m * share + HIGH] for h in range(KEPT)]
        evens, odds = [], []
        for h in range(0, KEPT, 2):
            evens.append(jnp.where(top, lines[h], pltpu.roll(lines[h + 1], share, 0)))
            odds.append(jnp.where(top, pltpu.roll(lines[h], share, 0), lines[h + 1]))
        part_out[m] = jnp.concatenate(evens, axis=0).astype(BF16)
        part_out[m + 1] = jnp.concatenate(odds, axis=0).astype(BF16)

    chunks = part_out.shape[0]
    from_slot = me // holders
    my_group = me // chunks

    def part_copy(m):
        return remote(
            part_out.at[m],
            part_in.at[from_slot],
            part_send.at[m],
            part_recv.at[from_slot],
            hold * chunks + m,
        )

    own_part = pltpu.make_async_copy(
        part_out.at[me % chunks], part_in.at[from_slot], part_recv.at[from_slot]
    )

    def start_part(m, carry):
        target = hold * chunks + m

        @pl.when(target != me)
        def _():
            part_copy(m).start()

        @pl.when(target == me)
        def _():
            own_part.start()

        return carry

    lax.fori_loop(0, chunks, start_part, 0)

    def end_part(i, carry):
        pltpu.make_async_copy(part_out.at[0], part_in.at[i], part_recv.at[i]).wait()
        return carry

    lax.fori_loop(0, chunks, end_part, 0)
    scale = (2.0 * SHARED) ** (-0.5)
    for p in range(2):
        total = part_in[p * quarter].astype(F32)
        for j in range(1, quarter):
            total += part_in[p * quarter + j].astype(F32)
        out[p] = (total * scale).astype(BF16)

    def end_part_send(m, carry):
        @pl.when(hold * chunks + m != me)
        def _():
            part_copy(m).wait_send()

        return carry

    lax.fori_loop(0, chunks, end_part_send, 0)
    for g in range(2):
        for name in names:
            gate_copy(g, name).wait_send()

    def end_deal(o, carry):
        deal_copy(o).wait_send()
        return carry

    lax.fori_loop(1, devices, end_deal, 0)

    def end_right_send(o, carry):
        right_copy(o).wait_send()
        return carry

    lax.fori_loop(1, in_pair, end_right_send, 0)
    for o in range(1, holders):
        left_copy(o).wait_send()


def run_whole(dealt, orders, gate_a, gate_b, devices):
    lines, width = dealt.shape[1:]
    depth = gate_a.shape[1]
    rows = devices * HIGH
    quarter = SHARED // width
    lot = devices * HIGH // 2 // KEPT
    chunks = devices // KEPT
    dma = pltpu.SemaphoreType.DMA
    vmem = pl.BlockSpec(memory_space=pltpu.VMEM)
    return pl.pallas_call(
        lambda *refs: whole_kernel(devices, *refs),
        out_shape=jax.ShapeDtypeStruct((2, lines, 2 * LANES), BF16),
        in_specs=[vmem] * 4,
        out_specs=vmem,
        scratch_shapes=[
            pltpu.VMEM((2, 2, 2, 2, 2, 2, 2, depth, width), BF16),
            pltpu.VMEM((devices, lines, width), BF16),
            pltpu.VMEM((2, rows, width), BF16),
            pltpu.VMEM((2, rows, width), F32),
            pltpu.VMEM((2, width, width), BF16),
            pltpu.VMEM((width, width), BF16),
            pltpu.VMEM((2, rows // 2, width), BF16),
            pltpu.VMEM((2, width // (LANES * KEPT), KEPT, rows // 2, LANES), BF16),
            pltpu.VMEM((2, KEPT, lot, width), BF16),
            pltpu.VMEM((quarter * KEPT, 2, width // (LANES * KEPT), lot, LANES), BF16),
            pltpu.VMEM((chunks, lines, 2 * LANES), BF16),
            pltpu.VMEM((chunks, lines, 2 * LANES), BF16),
            dma((5,)),
            dma((devices,)),
            dma((devices,)),
            dma((2, 11)),
            dma((2, 11)),
            dma((KEPT,)),
            dma((KEPT,)),
            dma((quarter * KEPT,)),
            dma((quarter * KEPT,)),
            dma((chunks,)),
            dma((chunks,)),
        ],
        compiler_params=pltpu.CompilerParams(
            collective_id=0, has_side_effects=True, vmem_limit_bytes=60 * 2**20
        ),
    )(dealt, orders, gate_a, gate_b)


def local(branch_in, column_order, gate_a, gate_b):
    join_scale = (2.0 * SHARED) ** (-0.5)
    devices = lax.axis_size("mode")
    me = lax.axis_index("mode")
    branches, parts, rows, width = branch_in.shape
    quarter = SHARED // width
    holders = devices // (2 * quarter)
    share = rows // (quarter * holders)
    pair = me // (quarter * holders)
    dealt = branch_in.reshape(2, 2, parts, holders, share, quarter, width)
    dealt = dealt.transpose(0, 5, 3, 2, 1, 4, 6).reshape(devices, parts, 2, share, width)
    orders = lax.dynamic_slice_in_dim(column_order, 2 * pair, 2, 0)
    lines = 2 * parts * share
    if lines == 2 * HIGH and holders == KEPT and devices == HIGH * KEPT == width // devices:
        done = run_whole(
            dealt.reshape(devices, lines, width), orders, gate_a, gate_b, devices
        )
        return done.reshape(2, lines, 2, LANES)
    whole_a = lax.all_gather(gate_a, "mode", axis=1, tiled=True)
    whole_b = lax.all_gather(gate_b, "mode", axis=1, tiled=True)
    dealt = lax.all_to_all(dealt, "mode", split_axis=0, concat_axis=0, tiled=True)
    state = dealt.transpose(1, 0, 2, 3, 4)
    state = layers_plain(state, orders, whole_a, whole_b)

    split = holders // KEPT
    piece = width // split
    free = devices * rows * width // (SHARED * KEPT)
    own_group = [
        [start * holders + h for h in range(holders)] for start in range(2 * quarter)
    ]
    pair_group = [
        [start * quarter * holders + d for d in range(quarter * holders)] for start in range(2)
    ]
    left = state[:, :, 0].reshape(parts, KEPT, devices // KEPT, share, split, piece)
    left = left.transpose(1, 4, 0, 2, 3, 5).reshape(
        holders, parts, devices // KEPT, share, piece
    )
    left = lax.all_to_all(
        left, "mode", split_axis=0, concat_axis=0, tiled=True, axis_index_groups=own_group
    )
    left = left.transpose(1, 2, 0, 3, 4).reshape(parts, free, piece)
    right = state[:, :, 1].reshape(parts, quarter, split, devices // (quarter * split), share, width)
    line = rows * width
    step = KEPT * free
    if width % step == 0:
        several = width // step
        right = right.reshape(
            parts, quarter, split, devices // (quarter * split), share, several, KEPT, free
        )
        right = right.transpose(1, 6, 2, 0, 3, 4, 5, 7)
        right = right.reshape(
            quarter * KEPT * split, parts, devices // (quarter * split), share, several, free
        )
        right = lax.all_to_all(
            right, "mode", split_axis=0, concat_axis=0, tiled=True, axis_index_groups=pair_group
        )
        right = right.reshape(
            quarter, holders, parts, devices // (quarter * split), share, several, free
        )
        right = right.transpose(2, 3, 1, 4, 0, 5, 6).reshape(parts, piece, free)
    else:
        spans = step // width
        kept_row = KEPT // spans
        right = right.reshape(
            parts, quarter, split, devices // (quarter * split), share, kept_row, free
        )
        own_j = me // holders % quarter
        g_high = own_j % spans
        slots = jnp.zeros(
            (quarter, spans, kept_row, split, parts, devices // (quarter * split), share, free), BF16
        )
        filled = right.transpose(1, 5, 2, 0, 3, 4, 6)
        slots = lax.dynamic_update_slice_in_dim(slots, filled[:, None], g_high, 1)
        slots = slots.reshape(
            quarter * KEPT * split, parts, devices // (quarter * split), share, free
        )
        slots = lax.all_to_all(
            slots, "mode", split_axis=0, concat_axis=0, tiled=True, axis_index_groups=pair_group
        )
        slots = slots.reshape(
            quarter // spans, spans, holders, parts, devices // (quarter * split), share, free
        )
        my_g = me % holders // split
        slots = lax.dynamic_index_in_dim(slots, my_g // kept_row, 1, keepdims=False)
        right = slots.transpose(2, 3, 1, 4, 0, 5).reshape(parts, piece, free)
    real_part, imag_part = complex_dot(left[0], left[1], right[0], right[1])
    partial = jnp.stack([real_part, imag_part], axis=1)
    return finish(partial, join_scale, devices, quarter, split)


def finish(partial, join_scale, devices, quarter, split):
    me = lax.axis_index("mode")
    free = partial.shape[0]
    holders = devices // (2 * quarter)
    sum_group = [
        [((p * quarter + j) * KEPT + g) * split + w for j in range(quarter) for w in range(split)]
        for p in range(2)
        for g in range(KEPT)
    ]
    count = quarter * split
    chunks = partial.astype(BF16).reshape(count, free // count, 2, free)
    chunks = lax.all_to_all(
        chunks, "mode", split_axis=0, concat_axis=0, tiled=True, axis_index_groups=sum_group
    )
    done = (jnp.sum(chunks.astype(F32), axis=0) * join_scale).astype(BF16)
    halves = done.reshape(2, free // (2 * count), 2, free)
    pair = me // (quarter * holders)
    same = lax.dynamic_index_in_dim(halves, pair, 0, keepdims=False)
    other = lax.dynamic_index_in_dim(halves, 1 - pair, 0, keepdims=False)
    same_pairs, other_pairs = [], []
    for d in range(devices):
        p, j, g, w = (
            d // (quarter * holders),
            d // holders % quarter,
            d // split % KEPT,
            d % split,
        )
        base = g * (devices // KEPT) + 2 * (j * split + w)
        same_pairs.append((d, base + p))
        other_pairs.append((d, base + 1 - p))
    from_same = lax.ppermute(same, "mode", same_pairs)
    from_other = lax.ppermute(other, "mode", other_pairs)
    parity = me % 2
    first = jnp.where(parity == 0, from_same, from_other)
    second = jnp.where(parity == 0, from_other, from_same)
    return jnp.stack([first, second])


def solution(mesh):
    in_specs = (
        P(None, None, ("cuts", "mode"), None),
        P(),
        P(None, "mode", None),
        P(None, "mode", None),
    )
    out_specs = P(None, ("cuts", "mode"), None, None)
    return jax.shard_map(local, mesh=mesh, in_specs=in_specs, out_specs=out_specs, check_vma=False)
```

profile of v0, /device:TPU:0, one launch (start us, length us, event | category | flops | bytes accessed | tf_op | source)
XLA Modules:
  0.0 116.5 jit_solution(13973795895083750680)
XLA Ops:
  0.0 0.0 copy-start
  0.0 1.5 %reshape.6 = bf16[2,2,2,4,4,4,1024]{6,5,4,3,2,1,0:T(4,128)(2,1)S(1)} reshape(bf16[4,2,64,1024]{3,2,1,0:T(8,128)(2,1)} %param.4) | data formatting | bytes 2097152 | tf_op jit(solution)/shard_map/reshape | solution.py:517
  1.5 0.6 copy.7
  2.1 1.1 reshape_reshape.3.refs_0_
  3.2 0.0 copy-done
  3.2 0.6 constant_dynamic-slice_fusion.refs_1_
  3.8 111.3 %shard_map.46 = bf16[2,16,256]{2,1,0:T(8,128)(2,1)} custom-call(bf16[32,16,1024]{2,1,0:T(8,128)(2,1)} %reshape_reshape.3.refs_0_, s32[2,1024]{1,0:T(2,128)} %constant_dynamic-slice_fusion.refs_1_, bf16[2,32,1024]{2,1,0:T(8,128)(2,1)} %refs_2_.1, bf16[2,32,1024]{2,1,0:T(8,128)(2,1)} %refs_3_.1), custom_call_target="tpu_custom_call" | custom-call | tf_op jit(solution)/shard_map/pallas_call | solution.py:472
  115.1 1.3 %reshape.7 = bf16[2,16,2,128]{3,2,1,0:T(2,128)(2,1)} reshape(bf16[2,16,256]{2,1,0:T(8,128)(2,1)} %shard_map.46) | data formatting | bytes 32768 | tf_op jit(solution)/shard_map/reshape | solution.py:525
Async XLA Ops:
  0.0 3.2 %copy-start = (s32[4,1024]{1,0:T(4,128)S(1)}, s32[4,1024]{1,0:T(4,128)}, u32[]{:S(2)}) copy-start(s32[4,1024]{1,0:T(4,128)} %param.5) | copy-start | bytes 49156
where the time goes:
time: 117 us; the launch traced here: 116 us
  Pallas kernels  111 us (95%)
  local copies, waits for them, and re-layouts  5.15 us (4%)
    pallas_call x1, Pallas kernels, run_whole(): pl.pallas_call(lambda *refs: whole_kernel(devices, *refs), out_shape=jax....  111 us

commit v1 on v0

--- a/solution.py
+++ b/solution.py
@@ -91,6 +91,8 @@
     deal_recv,
     gate_send,
     gate_recv,
+    line_send,
+    line_recv,
     left_send,
     left_recv,
     right_send,
@@ -124,49 +126,115 @@
             device_id_type=pl.DeviceIdType.MESH,
         )
 
-    z1, z0, y, x, c = (me // 16, me // 8 % 2, me // 4 % 2, me // 2 % 2, me % 2)
+    z, y, x, c = (me // 8, me // 4 % 2, me // 2 % 2, me % 2)
+    depth_z = devices // 8
+    half = depth_z // 2
     every = slice(None)
+    lower, higher = pl.ds(0, half), pl.ds(half, half)
     shards = (gate_a, gate_b)
     own = [
-        pltpu.make_async_copy(shards[g], gates.at[g, :, z1, z0, y, x, c], own_sem.at[g])
+        pltpu.make_async_copy(shards[g], gates.at[g, :, z, y, x, c], own_sem.at[g])
         for g in range(2)
     ]
     own_x = pltpu.make_async_copy(dealt.at[me], landed.at[me], own_sem.at[2])
     for copy in own + [own_x]:
         copy.start()
 
-    def region(g, part, index):
-        return gates.at[(g, part) + index]
-
-    steps = {
-        "z0": (every, (z1, z0, y, x, c), 8),
-        "z1": (every, (z1, every, y, x, c), 16),
-        "p0": (0, (every, every, y, x, c), 4),
-        "p1": (1, (every, every, y, x, c), 2),
-        "q0": (0, (every, every, every, x, c), 2),
-        "q1": (1, (every, every, y, every, c), 4),
-        "c0": (every, (every, every, y, x, c), 1),
-        "d0": (0, (every, every, 1 - y, x, c), 1),
-        "d1": (1, (every, every, y, 1 - x, c), 1),
-        "e0": (0, (every, every, every, 1 - x, c), 1),
-        "e1": (1, (every, every, 1 - y, every, c), 1),
-    }
-    names = list(steps)
-
-    def gate_copy(g, name):
-        part, index, bit = steps[name]
-        k = names.index(name)
-        here = region(g, part, index)
-        src = shards[g] if name == "z0" else here
+    swaps = (
+        {
+            "p0": (0, every, y, x, 4),
+            "p1": (1, every, y, x, 2),
+            "q0": (0, lower, every, x, 2),
+            "q1": (1, lower, y, every, 4),
+            "r0": (0, higher, every, x, 2),
+            "r1": (1, higher, y, every, 4),
+            "c0": (every, every, y, x, 1),
+            "d0": (0, every, 1 - y, x, 1),
+            "d1": (1, every, y, 1 - x, 1),
+            "e0": (0, lower, every, 1 - x, 1),
+            "e1": (1, lower, 1 - y, every, 1),
+            "f0": (0, higher, every, 1 - x, 1),
+            "f1": (1, higher, 1 - y, every, 1),
+        },
+        {
+            "p0": (0, z, y, x, 4),
+            "p1": (1, z, y, x, 2),
+            "q0": (0, lower, every, x, 2),
+            "q1": (1, lower, y, every, 4),
+            "r0": (0, higher, every, x, 2),
+            "r1": (1, higher, y, every, 4),
+            "d0": (0, every, every, x, 1),
+            "d1": (1, every, y, every, 1),
+            "e0": (0, lower, every, 1 - x, 1),
+            "e1": (1, lower, 1 - y, every, 1),
+            "f0": (0, higher, every, 1 - x, 1),
+            "f1": (1, higher, 1 - y, every, 1),
+        },
+    )
+
+    def swap_copy(g, name):
+        part, at_z, at_y, at_x, bit = swaps[g][name]
+        k = list(swaps[g]).index(name)
+        here = gates.at[g, part, at_z, at_y, at_x, c]
+        src = shards[1].at[part] if g == 1 and name in ("p0", "p1") else here
         return remote(src, here, gate_send.at[g, k], gate_recv.at[g, k], me ^ bit)
 
     def send(g, *which):
         for name in which:
-            gate_copy(g, name).start()
+            swap_copy(g, name).start()
 
     def arrive(g, *which):
         for name in which:
-            gate_copy(g, name).wait_recv()
+            swap_copy(g, name).wait_recv()
+
+    threads = ((0, every, y, x), (1, 0, every, x), (1, 1, y, every))
+
+    def line_copy(t, up, k):
+        g, part, at_y, at_x = threads[t]
+        block = z - k if up else z + k
+        here = gates.at[g, part, block, at_y, at_x, c]
+        src = shards[0] if t == 0 and k == 0 else here
+        n = (t * 2 + up) * (depth_z - 1) + k
+        return remote(
+            src, here, line_send.at[n], line_recv.at[n], me + 8 if up else me - 8
+        )
+
+    def line_sends(up, k):
+        return (z >= k) & (z < depth_z - 1) if up else (z + k < depth_z) & (z > 0)
+
+    def line_gets(up, k):
+        return z >= k + 1 if up else z + 1 + k < depth_z
+
+    def line_start(k, *which):
+        for up in (1, 0):
+
+            @pl.when(line_sends(up, k))
+            def _():
+                for t in which:
+                    line_copy(t, up, k).start()
+
+    def line_arrive(k, *which):
+        for up in (1, 0):
+
+            @pl.when(line_gets(up, k))
+            def _():
+                for t in which:
+                    g, part, at_y, at_x = threads[t]
+                    block = z - 1 - k if up else z + 1 + k
+                    here = gates.at[g, part, block, at_y, at_x, c]
+                    n = (t * 2 + up) * (depth_z - 1) + k
+                    remote(
+                        here, here, line_send.at[n], line_recv.at[n], me ^ 8
+                    ).wait_recv()
+
+    def line_end():
+        for t in range(len(threads)):
+            for up in (1, 0):
+                for k in range(depth_z - 1):
+
+                    @pl.when(line_sends(up, k))
+                    def _():
+                        line_copy(t, up, k).wait_send()
 
     def deal_copy(o):
         return remote(dealt.at[me ^ o], landed.at[me], deal_send.at[o], deal_recv.at[o], me ^ o)
@@ -176,31 +244,44 @@
         return carry
 
     pl.semaphore_wait(barrier, devices - 1)
-    send(0, "z0")
-    send(1, "z0")
+    line_start(0, 0)
+    send(1, "p0", "p1")
     lax.fori_loop(1, 8, start_deal, 0)
-    k = lax.broadcasted_iota(jnp.int32, (width, width), 1)
+    for copy in own:
+        copy.wait()
+    line_arrive(0, 0)
+    line_start(1, 0)
+    arrive(1, "p0", "p1")
+    line_start(0, 1, 2)
+    line_arrive(1, 0)
+    line_start(2, 0)
+    lax.fori_loop(8, 16, start_deal, 0)
+    line_arrive(2, 0)
+    send(0, "p0", "p1", "c0")
+    line_arrive(0, 1, 2)
+    line_start(1, 1, 2)
+    lax.fori_loop(16, 24, start_deal, 0)
+    arrive(0, "p0", "p1")
+    send(0, "q0", "q1", "r0", "r1", "d0", "d1")
+    line_arrive(1, 1, 2)
+    line_start(2, 1, 2)
+    lax.fori_loop(24, devices, start_deal, 0)
+    k = lax.broadcasted_iota(jnp.int32, (1, width), 1)
     natural = (
         (k % 32 // share) * 128 + (k // 64 % 4) * 32 + (k % share) * 8 + (k // 256) * 2 + k // 32 % 2
     )
-    for copy in own:
-        copy.wait()
-    arrive(0, "z0")
-    send(0, "z1")
-    arrive(1, "z0")
-    send(1, "z1")
-    lax.fori_loop(8, devices, start_deal, 0)
     mixer[...] = jnp.where(
         lax.broadcasted_iota(jnp.int32, (width, width), 0) == natural, 1.0, 0.0
     ).astype(BF16)
-    arrive(0, "z1")
-    send(0, "p0", "p1", "c0")
-    arrive(1, "z1")
-    send(1, "p0", "p1", "c0")
-    arrive(0, "p0", "p1")
-    send(0, "q0", "q1", "d0", "d1")
-    arrive(1, "p0", "p1")
-    send(1, "q0", "q1", "d0", "d1")
+    for side in range(2):
+        source = lax.broadcasted_iota(jnp.int32, (width, width), 0)
+        hot[side] = jnp.where(source == orders[side : side + 1, :], 1.0, 0.0).astype(BF16)
+    arrive(0, "q0", "q1")
+    send(0, "e0", "e1")
+    line_arrive(2, 1, 2)
+    send(1, "q0", "q1", "r0", "r1", "d0", "d1")
+    arrive(0, "r0", "r1")
+    send(0, "f0", "f1")
 
     own_x.wait()
 
@@ -213,9 +294,6 @@
     for part in range(2):
         state[part] = wide[:, part * HIGH : (part + 1) * HIGH].reshape(rows, width).astype(BF16)
     first_side = lax.broadcasted_iota(jnp.int32, (rows, width // 4), 0) % HIGH < share
-    for side in range(2):
-        source = lax.broadcasted_iota(jnp.int32, (width, width), 0)
-        hot[side] = jnp.where(source == orders[side : side + 1, :], 1.0, 0.0).astype(BF16)
 
     def tile_of(n):
         return pl.ds(pl.multiple_of(n * (width // 4), width // 4), width // 4)
@@ -235,8 +313,8 @@
         @pl.loop(0, 4)
         def _(n):
             cols = tile_of(n)
-            real = gates[g, 0, :, :, :, :, :, :, cols].reshape(width, width // 4)
-            imag = gates[g, 1, :, :, :, :, :, :, cols].reshape(width, width // 4)
+            real = gates[g, 0, :, :, :, :, :, cols].reshape(width, width // 4)
+            imag = gates[g, 1, :, :, :, :, :, cols].reshape(width, width // 4)
             real_part, imag_part = complex_dot(state[0], state[1], real, imag)
             product[0, :, cols] = real_part
             product[1, :, cols] = imag_part
@@ -257,14 +335,14 @@
                         blocks, axis=0
                     ).astype(BF16)
 
-    arrive(0, "q0", "q1")
-    send(0, "e0", "e1")
-    arrive(0, "c0", "d0", "d1", "e0", "e1")
+    arrive(0, "c0", "d0", "d1", "e0", "e1", "f0", "f1")
     layer(0)
     regroup()
     arrive(1, "q0", "q1")
     send(1, "e0", "e1")
-    arrive(1, "c0", "d0", "d1", "e0", "e1")
+    arrive(1, "r0", "r1")
+    send(1, "f0", "f1")
+    arrive(1, "d0", "d1", "e0", "e1", "f0", "f1")
     layer(1)
     for number in range(2, 2 * CYCLES):
         regroup()
@@ -442,8 +520,9 @@
 
     lax.fori_loop(0, chunks, end_part_send, 0)
     for g in range(2):
-        for name in names:
-            gate_copy(g, name).wait_send()
+        for name in swaps[g]:
+            swap_copy(g, name).wait_send()
+    line_end()
 
     def end_deal(o, carry):
         deal_copy(o).wait_send()
@@ -475,7 +554,7 @@
         in_specs=[vmem] * 4,
         out_specs=vmem,
         scratch_shapes=[
-            pltpu.VMEM((2, 2, 2, 2, 2, 2, 2, depth, width), BF16),
+            pltpu.VMEM((2, 2, devices // 8, 2, 2, 2, depth, width), BF16),
             pltpu.VMEM((devices, lines, width), BF16),
             pltpu.VMEM((2, rows, width), BF16),
             pltpu.VMEM((2, rows, width), F32),
@@ -490,8 +569,10 @@
             dma((5,)),
             dma((devices,)),
             dma((devices,)),
-            dma((2, 11)),
-            dma((2, 11)),
+            dma((2, 13)),
+            dma((2, 13)),
+            dma((6 * (devices // 8 - 1),)),
+            dma((6 * (devices // 8 - 1),)),
             dma((KEPT,)),
             dma((KEPT,)),
             dma((quarter * KEPT,)),

time: 117 us -> 101 us (0.86)
  Pallas kernels: 111 us -> 95.9 us
    pallas_call x1, Pallas kernels: 111 us -> 95.9 us  [run_whole(): pl.pallas_call(lambda *refs: whole_kernel(devices, *refs), out_shape=jax....]
where the time goes in v1:
time: 101 us
  Pallas kernels  95.9 us (95%)
  local copies, waits for them, and re-layouts  5.15 us (5%)
    pallas_call x1, Pallas kernels, run_whole(): pl.pallas_call(lambda *refs: whole_kernel(devices, *refs), out_shape=jax....  95.9 us
    reshape x2, local copies, waits for them, and re-layouts, local(): dealt = branch_in.reshape(2, 2, parts, holders, share, quarter, width)  2.08 us

profile of v1, /device:TPU:0, one launch (start us, length us, event | category | flops | bytes accessed | tf_op | source)
XLA Modules:
  0.0 101.1 jit_solution(13895286583359539038)
XLA Ops:
  0.0 0.0 copy-start
  0.0 1.5 %reshape.6 = bf16[2,2,2,4,4,4,1024]{6,5,4,3,2,1,0:T(4,128)(2,1)S(1)} reshape(bf16[4,2,64,1024]{3,2,1,0:T(8,128)(2,1)} %param.4) | data formatting | bytes 2097152 | tf_op jit(solution)/shard_map/reshape | solution.py:598
  1.5 0.6 copy.7
  2.1 1.1 %reshape_reshape.3.refs_0_ = bf16[32,16,1024]{2,1,0:T(8,128)(2,1)} reshape(bf16[2,4,4,2,2,4,1024]{6,5,4,3,2,1,0:T(4,128)(2,1)S(1)} %bitcast.5) | data formatting | bytes 2097152 | tf_op jit(solution)/shard_map/reshape;reshape | solution.py:604
  3.2 0.0 copy-done
  3.2 0.6 constant_dynamic-slice_fusion.refs_1_
  3.8 95.9 %shard_map.46 = bf16[2,16,256]{2,1,0:T(8,128)(2,1)} custom-call(bf16[32,16,1024]{2,1,0:T(8,128)(2,1)} %reshape_reshape.3.refs_0_, s32[2,1024]{1,0:T(2,128)} %constant_dynamic-slice_fusion.refs_1_, bf16[2,32,1024]{2,1,0:T(8,128)(2,1)} %refs_2_.1, bf16[2,32,1024]{2,1,0:T(8,128)(2,1)} %refs_3_.1), custom_call_target="tpu_custom_call" | custom-call | tf_op jit(solution)/shard_map/pallas_call | solution.py:551
  99.7 1.3 %reshape.7 = bf16[2,16,2,128]{3,2,1,0:T(2,128)(2,1)} reshape(bf16[2,16,256]{2,1,0:T(8,128)(2,1)} %shard_map.46) | data formatting | bytes 32768 | tf_op jit(solution)/shard_map/reshape | solution.py:606
Async XLA Ops:
  0.0 3.2 %copy-start = (s32[4,1024]{1,0:T(4,128)S(1)}, s32[4,1024]{1,0:T(4,128)}, u32[]{:S(2)}) copy-start(s32[4,1024]{1,0:T(4,128)} %param.5) | copy-start | bytes 49156

commit v2 on v1

--- a/solution.py
+++ b/solution.py
@@ -128,9 +128,7 @@
 
     z, y, x, c = (me // 8, me // 4 % 2, me // 2 % 2, me % 2)
     depth_z = devices // 8
-    half = depth_z // 2
     every = slice(None)
-    lower, higher = pl.ds(0, half), pl.ds(half, half)
     shards = (gate_a, gate_b)
     own = [
         pltpu.make_async_copy(shards[g], gates.at[g, :, z, y, x, c], own_sem.at[g])
@@ -142,50 +140,75 @@
 
     swaps = (
         {
-            "p0": (0, every, y, x, 4),
-            "p1": (1, every, y, x, 2),
-            "q0": (0, lower, every, x, 2),
-            "q1": (1, lower, y, every, 4),
-            "r0": (0, higher, every, x, 2),
-            "r1": (1, higher, y, every, 4),
-            "c0": (every, every, y, x, 1),
-            "d0": (0, every, 1 - y, x, 1),
-            "d1": (1, every, y, 1 - x, 1),
-            "e0": (0, lower, every, 1 - x, 1),
-            "e1": (1, lower, 1 - y, every, 1),
-            "f0": (0, higher, every, 1 - x, 1),
-            "f1": (1, higher, 1 - y, every, 1),
+            "p0": (0, y, x, 4),
+            "p1": (1, y, x, 2),
+            "q0": (0, every, x, 2),
+            "q1": (1, y, every, 4),
+            "c0": (every, y, x, 1),
+            "d0": (0, 1 - y, x, 1),
+            "d1": (1, y, 1 - x, 1),
+            "e0": (0, every, 1 - x, 1),
+            "e1": (1, 1 - y, every, 1),
         },
         {
-            "p0": (0, z, y, x, 4),
-            "p1": (1, z, y, x, 2),
-            "q0": (0, lower, every, x, 2),
-            "q1": (1, lower, y, every, 4),
-            "r0": (0, higher, every, x, 2),
-            "r1": (1, higher, y, every, 4),
-            "d0": (0, every, every, x, 1),
-            "d1": (1, every, y, every, 1),
-            "e0": (0, lower, every, 1 - x, 1),
-            "e1": (1, lower, 1 - y, every, 1),
-            "f0": (0, higher, every, 1 - x, 1),
-            "f1": (1, higher, 1 - y, every, 1),
+            "q0": (0, every, x, 2),
+            "q1": (1, y, every, 4),
+            "d0": (0, every, x, 1),
+            "d1": (1, y, every, 1),
+            "e0": (0, every, 1 - x, 1),
+            "e1": (1, 1 - y, every, 1),
+            "p0": (0, y, x, 4),
+            "p1": (1, y, x, 2),
         },
     )
 
-    def swap_copy(g, name):
-        part, at_z, at_y, at_x, bit = swaps[g][name]
+    def swap_copy(g, name, place):
+        part, at_y, at_x, bit = swaps[g][name]
         k = list(swaps[g]).index(name)
-        here = gates.at[g, part, at_z, at_y, at_x, c]
-        src = shards[1].at[part] if g == 1 and name in ("p0", "p1") else here
-        return remote(src, here, gate_send.at[g, k], gate_recv.at[g, k], me ^ bit)
-
-    def send(g, *which):
-        for name in which:
-            swap_copy(g, name).start()
-
-    def arrive(g, *which):
-        for name in which:
-            swap_copy(g, name).wait_recv()
+        here = gates.at[g, part, z + place, at_y, at_x, c]
+        first = name in ("p0", "p1", "c0") and place == 0
+        src = (shards[g] if name == "c0" else shards[g].at[part]) if first else here
+        n = place + depth_z - 1
+        return remote(src, here, gate_send.at[g, k, n], gate_recv.at[g, k, n], me ^ bit)
+
+    def on_round(r, action):
+        for place in (0,) if r == 0 else (-r, r):
+            if place == 0:
+                action(place)
+            else:
+
+                @pl.when((z + place >= 0) & (z + place < depth_z))
+                def _():
+                    action(place)
+
+    def send(g, r, *which):
+        def action(place):
+            for name in which:
+                swap_copy(g, name, place).start()
+
+        on_round(r, action)
+
+    def pass_on(g, r, got, which):
+        def action(place):
+            for name in got:
+                swap_copy(g, name, place).wait_recv()
+            for name in which:
+                swap_copy(g, name, place).start()
+
+        on_round(r, action)
+
+    def swaps_end(g, recv, *which):
+        for r in range(depth_z):
+
+            def action(place):
+                for name in which:
+                    copy = swap_copy(g, name, place)
+                    if recv is True:
+                        copy.wait_recv()
+                    else:
+                        copy.wait_send()
+
+            on_round(r, action)
 
     threads = ((0, every, y, x), (1, 0, every, x), (1, 1, y, every))
 
@@ -244,28 +267,53 @@
         return carry
 
     pl.semaphore_wait(barrier, devices - 1)
+    through = ("q0", "q1", "d0", "d1")
+    start = ("p0", "p1", "c0")
+
+    def first_a(r):
+        line_arrive(r - 1, 0)
+        if r < depth_z - 1:
+            line_start(r, 0)
+        send(0, r, *start)
+
+    def second_a(r):
+        pass_on(0, r, ("p0", "p1"), through)
+
+    def third(g, r):
+        pass_on(g, r, ("q0", "q1"), ("e0", "e1"))
+
+    def first_b(r):
+        line_arrive(r - 1, 1, 2)
+        if r < depth_z - 1:
+            line_start(r, 1, 2)
+        send(1, r, *through)
+
     line_start(0, 0)
-    send(1, "p0", "p1")
-    lax.fori_loop(1, 8, start_deal, 0)
+    send(1, 0, "p0", "p1")
+    send(0, 0, *start)
     for copy in own:
         copy.wait()
-    line_arrive(0, 0)
-    line_start(1, 0)
-    arrive(1, "p0", "p1")
+    pass_on(1, 0, ("p0", "p1"), ())
     line_start(0, 1, 2)
-    line_arrive(1, 0)
-    line_start(2, 0)
-    lax.fori_loop(8, 16, start_deal, 0)
-    line_arrive(2, 0)
-    send(0, "p0", "p1", "c0")
-    line_arrive(0, 1, 2)
-    line_start(1, 1, 2)
-    lax.fori_loop(16, 24, start_deal, 0)
-    arrive(0, "p0", "p1")
-    send(0, "q0", "q1", "r0", "r1", "d0", "d1")
-    line_arrive(1, 1, 2)
-    line_start(2, 1, 2)
-    lax.fori_loop(24, devices, start_deal, 0)
+    first_a(1)
+    second_a(0)
+    send(1, 0, *through)
+    lax.fori_loop(1, 12, start_deal, 0)
+    first_a(2)
+    first_b(1)
+    second_a(1)
+    lax.fori_loop(12, 20, start_deal, 0)
+    first_a(3)
+    third(0, 0)
+    second_a(2)
+    first_b(2)
+    lax.fori_loop(20, devices, start_deal, 0)
+    third(1, 0)
+    third(0, 1)
+    second_a(3)
+    first_b(3)
+    third(1, 1)
+    third(0, 2)
     k = lax.broadcasted_iota(jnp.int32, (1, width), 1)
     natural = (
         (k % 32 // share) * 128 + (k // 64 % 4) * 32 + (k % share) * 8 + (k // 256) * 2 + k // 32 % 2
@@ -276,13 +324,8 @@
     for side in range(2):
         source = lax.broadcasted_iota(jnp.int32, (width, width), 0)
         hot[side] = jnp.where(source == orders[side : side + 1, :], 1.0, 0.0).astype(BF16)
-    arrive(0, "q0", "q1")
-    send(0, "e0", "e1")
-    line_arrive(2, 1, 2)
-    send(1, "q0", "q1", "r0", "r1", "d0", "d1")
-    arrive(0, "r0", "r1")
-    send(0, "f0", "f1")
-
+    third(0, 3)
+    third(1, 2)
     own_x.wait()
 
     def wait_deal(o, carry):
@@ -335,14 +378,11 @@
                         blocks, axis=0
                     ).astype(BF16)
 
-    arrive(0, "c0", "d0", "d1", "e0", "e1", "f0", "f1")
+    swaps_end(0, True, "c0", "d0", "d1", "e0", "e1")
     layer(0)
     regroup()
-    arrive(1, "q0", "q1")
-    send(1, "e0", "e1")
-    arrive(1, "r0", "r1")
-    send(1, "f0", "f1")
-    arrive(1, "d0", "d1", "e0", "e1", "f0", "f1")
+    third(1, 3)
+    swaps_end(1, True, "d0", "d1", "e0", "e1")
     layer(1)
     for number in range(2, 2 * CYCLES):
         regroup()
@@ -519,9 +559,10 @@
         return carry
 
     lax.fori_loop(0, chunks, end_part_send, 0)
-    for g in range(2):
-        for name in swaps[g]:
-            swap_copy(g, name).wait_send()
+    swaps_end(0, False, *swaps[0])
+    swaps_end(1, False, *list(swaps[1])[:6])
+    for name in ("p0", "p1"):
+        swap_copy(1, name, 0).wait_send()
     line_end()
 
     def end_deal(o, carry):
@@ -569,8 +610,8 @@
             dma((5,)),
             dma((devices,)),
             dma((devices,)),
-            dma((2, 13)),
-            dma((2, 13)),
+            dma((2, 9, 2 * (devices // 8) - 1)),
+            dma((2, 9, 2 * (devices // 8) - 1)),
             dma((6 * (devices // 8 - 1),)),
             dma((6 * (devices // 8 - 1),)),
             dma((KEPT,)),

time: 101 us -> 101 us (level)
  no operation moved by 1% of the time
where the time goes in v2:
time: 101 us; the launch traced here: 100 us
  Pallas kernels  95.1 us (94%)
  local copies, waits for them, and re-layouts  5.15 us (5%)
    pallas_call x1, Pallas kernels, run_whole(): pl.pallas_call(lambda *refs: whole_kernel(devices, *refs), out_shape=jax....  95.1 us
    reshape x2, local copies, waits for them, and re-layouts, local(): dealt = branch_in.reshape(2, 2, parts, holders, share, quarter, width)  2.08 us

profile of v2, /device:TPU:0, one launch (start us, length us, event | category | flops | bytes accessed | tf_op | source)
XLA Modules:
  0.0 100.3 jit_solution(375502256385702719)
XLA Ops:
  0.0 0.0 copy-start
  0.0 1.5 %reshape.6 = bf16[2,2,2,4,4,4,1024]{6,5,4,3,2,1,0:T(4,128)(2,1)S(1)} reshape(bf16[4,2,64,1024]{3,2,1,0:T(8,128)(2,1)} %param.4) | data formatting | bytes 2097152 | tf_op jit(solution)/shard_map/reshape | solution.py:639
  1.5 0.6 copy.7
  2.1 1.1 %reshape_reshape.3.refs_0_ = bf16[32,16,1024]{2,1,0:T(8,128)(2,1)} reshape(bf16[2,4,4,2,2,4,1024]{6,5,4,3,2,1,0:T(4,128)(2,1)S(1)} %bitcast.5) | data formatting | bytes 2097152 | tf_op jit(solution)/shard_map/reshape;reshape | solution.py:645
  3.2 0.0 copy-done
  3.2 0.6 constant_dynamic-slice_fusion.refs_1_
  3.8 95.1 %shard_map.46 = bf16[2,16,256]{2,1,0:T(8,128)(2,1)} custom-call(bf16[32,16,1024]{2,1,0:T(8,128)(2,1)} %reshape_reshape.3.refs_0_, s32[2,1024]{1,0:T(2,128)} %constant_dynamic-slice_fusion.refs_1_, bf16[2,32,1024]{2,1,0:T(8,128)(2,1)} %refs_2_.1, bf16[2,32,1024]{2,1,0:T(8,128)(2,1)} %refs_3_.1), custom_call_target="tpu_custom_call" | custom-call | tf_op jit(solution)/shard_map/pallas_call | solution.py:592
  98.9 1.3 %reshape.7 = bf16[2,16,2,128]{3,2,1,0:T(2,128)(2,1)} reshape(bf16[2,16,256]{2,1,0:T(8,128)(2,1)} %shard_map.46) | data formatting | bytes 32768 | tf_op jit(solution)/shard_map/reshape | solution.py:647
Async XLA Ops:
  0.0 3.2 %copy-start = (s32[4,1024]{1,0:T(4,128)S(1)}, s32[4,1024]{1,0:T(4,128)}, u32[]{:S(2)}) copy-start(s32[4,1024]{1,0:T(4,128)} %param.5) | copy-start | bytes 49156
